TPU v7x, 32 devices: a whole 2x2x4 slice. The times are simulated.
32 devices in a mesh: grp: 2 (over x), gx: 16 (over z, y, core).
Axes of the slice: x: 2, y: 2, z: 4, core: 2. Of those that a mesh axis runs over, the one named last changes fastest.
Arguments:
- grain_ids: int32 [96, 32, 512], P(('grp', 'gx')), parts along dimension 0, may hold values from 0 to 7
- jitter: bfloat16 [8, 96, 32, 512], P(None, ('grp', 'gx')), parts along dimension 1, may hold values from 0 to 0.5
- class_table: int32 [8, 8], replicated, may hold values from 0 to 3
- chosen: int32 [2], replicated, may hold values from 0 to 7
Outputs:
- order_params: float32 [8, 96, 32, 512], P(None, ('grp', 'gx')), parts along dimension 1
- correlation: float32 [2, 96, 32, 512], P(None, ('grp', 'gx')), parts along dimension 1
There are 2 independent parts, one for each index of `grp`. A program takes and returns all parts, laid end to end along the dimension named above; an argument that names none is the same for every part. Nothing has to cross between parts.
All inputs are finite; a program needn't handle non-finite values.
Results may differ from a plain program's by a relative error of at most 0.0003.
Values sent between devices are 32-bit elements; how exact they have to be, the bound alone decides.
No kernel may reach another device: no remote copies, remote signals or barrier semaphores. Data moves between devices by JAX's collectives and lax.ppermute only.
A program may use at most 128 MiB of HBM per device.

v0:
```python
import math
import jax
import jax.numpy as jnp
from jax import lax
from jax.sharding import PartitionSpec as P

STEPS = 3
HIGH = lax.Precision.HIGHEST


def with_halo(value, sides, width):
    for axis, dim in sides:
        peers, length = (lax.axis_size(axis), value.shape[dim])
        up = [(i, (i + 1) % peers) for i in range(peers)]
        down = [(j, i) for i, j in up]
        last = lax.slice_in_dim(value, length - width, length, axis=dim)
        initial = lax.slice_in_dim(value, 0, width, axis=dim)
        before = lax.ppermute(last, axis, up)
        after = lax.ppermute(initial, axis, down)
        value = jnp.concatenate([before, value, after], axis=dim)
    return value


def tables(length):
    index = lax.iota(jnp.int32, length)
    product = index[:, None] * index[None, :] % length
    angle = product.astype(jnp.float32) * (2.0 * math.pi / length)
    return (jnp.cos(angle), jnp.sin(angle))


def onehot_of(grain_ids):
    return (grain_ids[None] == lax.iota(jnp.int32, 8)[:, None, None, None]).astype(jnp.float32)


def levels_map(onehot, class_table):
    levels = 0.4 + 0.2 * class_table.astype(jnp.float32)
    return jnp.einsum("gi,gxzy->ixzy", levels, onehot, precision=HIGH)


def advance(extended, mobility):
    center = extended[:, 1:-1]
    lap = extended[:, 2:] + extended[:, :-2]
    lap = lap + jnp.roll(center, -1, 2) + jnp.roll(center, 1, 2)
    lap = lap + jnp.roll(center, -1, 3) + jnp.roll(center, 1, 3)
    lap = lap - 6.0 * center
    total = jnp.sum(center * center, axis=0)
    drive = -center + center * center * center + 3.0 * center * (total[None] - center * center)
    return center - 0.12 * mobility * (drive - lap)


def forward_planes(fields, cos_y, sin_y, cos_z, sin_z):
    real_y = jnp.dot(fields, cos_y, precision=HIGH)
    imag_y = -jnp.dot(fields, sin_y, precision=HIGH)
    real_z = jnp.einsum("kz,fxzy->fxky", cos_z, real_y, precision=HIGH) + jnp.einsum(
        "kz,fxzy->fxky", sin_z, imag_y, precision=HIGH
    )
    imag_z = jnp.einsum("kz,fxzy->fxky", cos_z, imag_y, precision=HIGH) - jnp.einsum(
        "kz,fxzy->fxky", sin_z, real_y, precision=HIGH
    )
    planes = fields.shape[1]
    return (
        real_z.reshape(fields.shape[0], planes, -1),
        imag_z.reshape(fields.shape[0], planes, -1),
    )


def line_power(real_part, imag_part, cos_x, sin_x, offset):
    real_x = jnp.einsum("kx,fxc->fkc", cos_x, real_part, precision=HIGH) + jnp.einsum(
        "kx,fxc->fkc", sin_x, imag_part, precision=HIGH
    )
    imag_x = jnp.einsum("kx,fxc->fkc", cos_x, imag_part, precision=HIGH) - jnp.einsum(
        "kx,fxc->fkc", sin_x, real_part, precision=HIGH
    )
    power = real_x * real_x + imag_x * imag_x
    freq_x = lax.iota(jnp.int32, power.shape[1])[:, None]
    column = offset + lax.iota(jnp.int32, power.shape[2])[None, :]
    keep = jnp.logical_not(jnp.logical_and(freq_x == 0, column == 0))
    power = power * keep.astype(jnp.float32)[None]
    back_real = jnp.einsum("kx,fkc->fxc", cos_x, power, precision=HIGH)
    back_imag = jnp.einsum("kx,fkc->fxc", sin_x, power, precision=HIGH)
    return (back_real, back_imag)


def inverse_planes(back_real, back_imag, cos_y, sin_y, cos_z, sin_z, depth, width, count):
    fields = back_real.shape[0]
    planes = back_real.shape[1]
    back_real = back_real.reshape(fields, planes, depth, width)
    back_imag = back_imag.reshape(fields, planes, depth, width)
    real_z = jnp.einsum("kz,fxky->fxzy", cos_z, back_real, precision=HIGH) - jnp.einsum(
        "kz,fxky->fxzy", sin_z, back_imag, precision=HIGH
    )
    imag_z = jnp.einsum("kz,fxky->fxzy", cos_z, back_imag, precision=HIGH) + jnp.einsum(
        "kz,fxky->fxzy", sin_z, back_real, precision=HIGH
    )
    result = jnp.dot(real_z, cos_y, precision=HIGH) - jnp.dot(imag_z, sin_y, precision=HIGH)
    return result / (count * count)


def shards(grain_ids, jitter, class_table, chosen):
    planes = grain_ids.shape[0]
    depth = grain_ids.shape[1]
    width = grain_ids.shape[2]
    devices = lax.axis_size("gx")
    onehot = onehot_of(grain_ids)
    eta = 0.6 * onehot + jitter.astype(jnp.float32)
    mobility = levels_map(onehot, class_table)
    for step in range(STEPS):
        extended = with_halo(eta, (("gx", 1),), 1)
        eta = advance(extended, mobility)
    select = (chosen[:, None] == lax.iota(jnp.int32, 8)[None, :]).astype(jnp.float32)
    fields = jnp.einsum("ki,ixzy->kxzy", select, eta, precision=HIGH)
    cos_y, sin_y = tables(width)
    cos_z, sin_z = tables(depth)
    total_x = planes * devices
    cos_x, sin_x = tables(total_x)
    count = float(total_x * depth * width)
    columns = depth * width // devices
    offset = lax.axis_index("gx") * columns
    real_part, imag_part = forward_planes(fields, cos_y, sin_y, cos_z, sin_z)
    stacked = jnp.concatenate([real_part, imag_part], axis=0)
    lines = lax.all_to_all(stacked, "gx", split_axis=2, concat_axis=1, tiled=True)
    back_real, back_imag = line_power(lines[:2], lines[2:], cos_x, sin_x, offset)
    returned = lax.all_to_all(
        jnp.concatenate([back_real, back_imag], axis=0),
        "gx",
        split_axis=1,
        concat_axis=2,
        tiled=True,
    )
    correlation = inverse_planes(
        returned[:2], returned[2:], cos_y, sin_y, cos_z, sin_z, depth, width, count
    )
    return (eta, correlation)


def solution(mesh):
    in_specs = (P(("grp", "gx"), None, None), P(None, ("grp", "gx"), None, None), P(), P())
    out_specs = (P(None, ("grp", "gx"), None, None), P(None, ("grp", "gx"), None, None))
    return jax.shard_map(shards, mesh=mesh, in_specs=in_specs, out_specs=out_specs, check_vma=False)
```

profile of v0, /device:TPU:11, one launch (start us, length us, event | category | flops | bytes accessed | tf_op | source)
XLA Modules:
  0.0 307.3 jit_solution(3220175203014402098)
XLA Ops:
  0.6 1.8 convert_add_fusion
  2.5 0.7 collective-permute-start
  3.3 1.2 collective-permute-start.1
  4.5 0.4 fusion.241
  5.1 14.7 %multiply_subtract_fusion.2 = f32[8,3,32,512]{3,0,2,1:T(8,128)S(1)} fusion(bf16[8,3,32,512]{3,2,1,0:T(8,128)(2,1)S(1)} %copy-done.1, s32[3,32,512]{2,1,0:T(8,128)S(1)} %copy-done), kind=kOutput, calls=%fused_computation.12 | output fusion | flops 4374535 | bytes 2555904 | tf_op jit(solution)/shard_map/sub | solution.py:47
  19.9 0.6 fusion.239
  20.6 2.2 fusion.16
  22.8 0.4 fusion.236
  23.7 1.6 collective-permute-start.3
  25.3 0.6 fusion.234
  25.9 11.9 %collective-permute-done.2 = f32[8,1,32,512]{3,0,2,1:T(8,128)S(1)} collective-permute-done((f32[8,1,32,512]{3,0,2,1:T(8,128)S(1)}, f32[8,1,32,512]{3,0,2,1:T(8,128)S(1)}, u32[]{:S(2)}, u32[]{:S(2)}) %collective-permute-start.2) | collective-permute-done | bytes 524320 | tf_op jit(solution)/shard_map/ppermute | solution.py:19
  37.8 34.6 %fusion.21 = f32[8,3,32,512]{3,0,2,1:T(8,128)S(1)} fusion(f32[8,3,32,512]{3,0,2,1:T(8,128)S(1)} %get-tuple-element.42, f32[8,3,32,512]{3,0,2,1:T(8,128)S(1)} %get-tuple-element.43, f32[8,1,32,512]{3,0,2,1:T(8,128)S(1)} %collective-permute-done.3, f32[8,1,32,512]{3,0,2,1:T(8,128)S(1)} %collective-permute-done.2, f32[8,3,1,512]{3,0,2,1:T(8,128)S(1)} %get-tuple-element.23, ...), kind=kOutput, calls=%fused_computation.24 | output fusion | flops 9879559 | bytes 12058624 | tf_op jit(solution)/shard_map/sub | solution.py:47
  72.4 0.4 fusion.231
  73.2 2.3 collective-permute-start.5
  75.4 0.6 fusion.229
  76.0 11.4 %collective-permute-done.4 = f32[8,1,32,512]{3,0,2,1:T(8,128)S(1)} collective-permute-done((f32[8,1,32,512]{3,0,2,1:T(8,128)S(1)}, f32[8,1,32,512]{3,0,2,1:T(8,128)S(1)}, u32[]{:S(2)}, u32[]{:S(2)}) %collective-permute-start.4) | collective-permute-done | bytes 524320 | tf_op jit(solution)/shard_map/ppermute | solution.py:19
  87.4 34.6 %fusion.26 = f32[8,3,32,512]{3,0,2,1:T(8,128)S(1)} fusion(f32[8,3,32,512]{3,0,2,1:T(8,128)S(1)} %fusion.21, f32[8,3,32,512]{3,0,2,1:T(8,128)S(1)} %get-tuple-element.43, f32[8,1,32,512]{3,0,2,1:T(8,128)S(1)} %collective-permute-done.5, f32[8,1,32,512]{3,0,2,1:T(8,128)S(1)} %collective-permute-done.4, f32[8,3,1,512]{3,0,2,1:T(8,128)S(1)} %get-tuple-element.13, ...), kind=kOutput, calls=%fused_computation.29 | output fusion | flops 9879559 | bytes 12058624 | tf_op jit(solution)/shard_map/sub | solution.py:47
  122.1 0.9 fusion.155
  122.9 5.1 %fusion.62 = f32[2,3,32,512]{3,2,1,0:T(8,128)S(1)} fusion(f32[2,3,32,512]{3,0,2,1:T(2,128)S(1)} %fusion.155), kind=kOutput, calls=%fused_computation.86 | convolution fusion | flops 607649792 | bytes 786432 | tf_op jit(solution)/shard_map/dot_general | solution.py:52
  128.1 5.1 %convolution_negate_fusion = f32[2,3,32,512]{3,2,1,0:T(8,128)S(1)} fusion(f32[2,3,32,512]{3,0,2,1:T(2,128)S(1)} %fusion.155), kind=kOutput, calls=%fused_computation.76 | convolution fusion | flops 607748096 | bytes 786432 | tf_op jit(solution)/shard_map/dot_general | solution.py:53
  133.2 0.6 fusion.116
  133.8 0.6 fusion.114
  134.4 0.6 fusion.52
  135.3 0.6 fusion.51
  136.7 20.3 %copy.46 = f32[4,3,16384]{0,1,2:T(4,128)} copy(f32[4,3,16384]{2,0,1:T(4,128)S(1)} %pad_maximum_fusion.6) | data formatting | bytes 1572864 | tf_op jit(solution)/shard_map/concatenate | solution.py:120
  157.0 24.8 %reshape.88 = f32[16,1,12288]{2,1,0:T(1,128)} reshape(f32[16384,3,4]{2,1,0:T(4,128)} %bitcast.118) | data formatting | bytes 1572864
  181.8 7.3 %all-to-all-start = ((f32[16,1,12288]{2,1,0:T(1,128)}), f32[16,1,12288]{2,1,0:T(1,128)S(1)}, u32[]{:S(2)}, u32[]{:S(2)}) async-start(f32[16,1,12288]{2,1,0:T(1,128)} %reshape.88), calls=%async_computation | async-start | bytes 1572864 | tf_op jit(solution)/shard_map/all_to_all | solution.py:121
  189.3 19.3 %all-to-all-done = f32[16,1,12288]{2,1,0:T(1,128)S(1)} async-done(((f32[16,1,12288]{2,1,0:T(1,128)}), f32[16,1,12288]{2,1,0:T(1,128)S(1)}, u32[]{:S(2)}, u32[]{:S(2)}) %all-to-all-start) | async-done | bytes 786464 | tf_op jit(solution)/shard_map/all_to_all | solution.py:121
  208.6 0.5 broadcast.133
  209.1 2.5 reduce
  211.6 33.0 %reshape.89 = f32[16384,3,4]{2,1,0:T(4,128)} reshape(f32[16,12288]{1,0:T(8,128)S(1)} %reduce) | data formatting | bytes 1572864
  244.7 18.5 %copy.81 = f32[4,3,16,1024]{3,2,0,1:T(8,128)S(1)} copy(f32[4,3,16,1024]{0,1,3,2:T(4,128)} %bitcast.119) | data formatting | bytes 1572864 | tf_op jit(solution)/shard_map/all_to_all | solution.py:121
  263.6 0.7 fusion.76
  264.6 0.7 fusion.80
  265.2 0.7 fusion.49
  265.9 0.7 fusion.55
  266.7 0.6 convolution_bitcast_fusion
  267.2 0.6 convolution_bitcast_fusion.1
  267.9 1.4 copy.58
  269.3 4.6 %all-to-all-start.1 = ((f32[4,48,1024]{2,0,1:T(4,128)}), f32[4,48,1024]{2,0,1:T(4,128)S(1)}, u32[]{:S(2)}, u32[]{:S(2)}) async-start(f32[4,48,1024]{2,0,1:T(4,128)} %copy.58), calls=%async_computation.1 | async-start | bytes 1572864 | tf_op jit(solution)/shard_map/all_to_all | solution.py:123
  273.9 2.1 copy.61
  276.0 17.5 %all-to-all-done.1 = f32[4,48,1024]{2,0,1:T(4,128)S(1)} async-done(((f32[4,48,1024]{2,0,1:T(4,128)}), f32[4,48,1024]{2,0,1:T(4,128)S(1)}, u32[]{:S(2)}, u32[]{:S(2)}) %all-to-all-start.1) | async-done | bytes 786464 | tf_op jit(solution)/shard_map/all_to_all | solution.py:123
  294.0 0.5 fusion.110
  294.8 0.5 fusion.112
  295.3 0.6 fusion.47
  295.9 0.6 fusion.48
  296.4 5.1 %fusion.60 = f32[2,3,32,512]{3,2,1,0:T(8,128)S(1)} fusion(f32[2,3,32,512]{3,2,1,0:T(8,128)S(1)} %fusion.48), kind=kOutput, calls=%fused_computation.84 | convolution fusion | flops 607649792 | bytes 786432 | tf_op jit(solution)/shard_map/dot_general | solution.py:95
  301.5 5.6 %fusion.56 = f32[2,3,32,512]{3,2,1,0:T(8,128)} fusion(f32[2,3,32,512]{3,2,1,0:T(8,128)S(1)} %fusion.60, f32[2,3,32,512]{3,2,1,0:T(8,128)S(1)} %fusion.47), kind=kOutput, calls=%fused_computation.80 | convolution fusion | flops 607846400 | bytes 1179648 | tf_op jit(solution)/shard_map/dot_general | solution.py:95
  (40 shorter events, 3.7 us)
Async XLA Ops:
  2.5 17.9 %collective-permute-start = (f32[8,1,32,512]{3,0,2,1:T(8,128)S(1)}, f32[8,1,32,512]{3,0,2,1:T(8,128)S(1)}, u32[]{:S(2)}, u32[]{:S(2)}) collective-permute-start(f32[8,1,32,512]{3,0,2,1:T(8,128)S(1)} %get-tuple-element.36), channel_id=1, source_target_pairs={{1,0},{2,1},{3,2},{4,3},{5,4},{6,5},{7,6},{8,7},{9,8},{10,9},{11,1... | collective-permute-start | bytes 1572872 | tf_op jit(solution)/shard_map/ppermute | solution.py:19
  3.2 1.8 copy-start
  3.2 1.8 copy-start.1
  3.3 17.2 %collective-permute-start.1 = (f32[8,1,32,512]{3,0,2,1:T(8,128)S(1)}, f32[8,1,32,512]{3,0,2,1:T(8,128)S(1)}, u32[]{:S(2)}, u32[]{:S(2)}) collective-permute-start(f32[8,1,32,512]{3,0,2,1:T(8,128)S(1)} %get-tuple-element.37), channel_id=1, source_target_pairs={{0,1},{1,2},{2,3},{3,4},{4,5},{5,6},{6,7},{7,8},{8,9},{9,10},{10,1... | collective-permute-start | bytes 1572872 | tf_op jit(solution)/shard_map/ppermute | solution.py:18
  19.9 0.7 copy-start.2
  23.5 14.3 %collective-permute-start.2 = (f32[8,1,32,512]{3,0,2,1:T(8,128)S(1)}, f32[8,1,32,512]{3,0,2,1:T(8,128)S(1)}, u32[]{:S(2)}, u32[]{:S(2)}) collective-permute-start(f32[8,1,32,512]{3,0,2,1:T(8,128)S(1)} %get-tuple-element.26), channel_id=1, source_target_pairs={{1,0},{2,1},{3,2},{4,3},{5,4},{6,5},{7,6},{8,7},{9,8},{10,9},{11,1... | collective-permute-start | bytes 1572872 | tf_op jit(solution)/shard_map/ppermute | solution.py:19
  23.7 14.1 %collective-permute-start.3 = (f32[8,1,32,512]{3,0,2,1:T(8,128)S(1)}, f32[8,1,32,512]{3,0,2,1:T(8,128)S(1)}, u32[]{:S(2)}, u32[]{:S(2)}) collective-permute-start(f32[8,1,32,512]{3,0,2,1:T(8,128)S(1)} %get-tuple-element.27), channel_id=1, source_target_pairs={{0,1},{1,2},{2,3},{3,4},{4,5},{5,6},{6,7},{7,8},{8,9},{9,10},{10,1... | collective-permute-start | bytes 1572872 | tf_op jit(solution)/shard_map/ppermute | solution.py:18
  73.1 14.3 %collective-permute-start.4 = (f32[8,1,32,512]{3,0,2,1:T(8,128)S(1)}, f32[8,1,32,512]{3,0,2,1:T(8,128)S(1)}, u32[]{:S(2)}, u32[]{:S(2)}) collective-permute-start(f32[8,1,32,512]{3,0,2,1:T(8,128)S(1)} %get-tuple-element.16), channel_id=1, source_target_pairs={{1,0},{2,1},{3,2},{4,3},{5,4},{6,5},{7,6},{8,7},{9,8},{10,9},{11,1... | collective-permute-start | bytes 1572872 | tf_op jit(solution)/shard_map/ppermute | solution.py:19
  73.2 14.2 %collective-permute-start.5 = (f32[8,1,32,512]{3,0,2,1:T(8,128)S(1)}, f32[8,1,32,512]{3,0,2,1:T(8,128)S(1)}, u32[]{:S(2)}, u32[]{:S(2)}) collective-permute-start(f32[8,1,32,512]{3,0,2,1:T(8,128)S(1)} %get-tuple-element.17), channel_id=1, source_target_pairs={{0,1},{1,2},{2,3},{3,4},{4,5},{5,6},{6,7},{7,8},{8,9},{9,10},{10,1... | collective-permute-start | bytes 1572872 | tf_op jit(solution)/shard_map/ppermute | solution.py:18
  87.4 34.7 %copy-start.3 = (s32[2]{0:T(128)S(1)}, s32[2]{0:T(128)}, u32[]{:S(2)}) copy-start(s32[2]{0:T(128)} %param.7) | copy-start | bytes 28
  181.8 26.8 %all-to-all-start = ((f32[16,1,12288]{2,1,0:T(1,128)}), f32[16,1,12288]{2,1,0:T(1,128)S(1)}, u32[]{:S(2)}, u32[]{:S(2)}) async-start(f32[16,1,12288]{2,1,0:T(1,128)} %reshape.88), calls=%async_computation | async-start | bytes 1572864 | tf_op jit(solution)/shard_map/all_to_all | solution.py:121
  269.3 24.2 %all-to-all-start.1 = ((f32[4,48,1024]{2,0,1:T(4,128)}), f32[4,48,1024]{2,0,1:T(4,128)S(1)}, u32[]{:S(2)}, u32[]{:S(2)}) async-start(f32[4,48,1024]{2,0,1:T(4,128)} %copy.58), calls=%async_computation.1 | async-start | bytes 1572864 | tf_op jit(solution)/shard_map/all_to_all | solution.py:123
where the time goes:
time: 313 us; the launch traced here: 307 us
  local copies, waits for them, and re-layouts  107 us (34%)
  other arithmetic  88.9 us (28%)
  waiting for transfers between devices  60.1 us (19%)
  matrix products  32.5 us (10%)
  starting transfers between devices  18 us (6%)
    sub x3, other arithmetic, advance(): total[None] - center * center  84 us
    unnamed x11, local copies, waits for them, and re-layouts  60 us
    ppermute x3, waiting for transfers between devices, with_halo(): after = lax.ppermute(initial, axis, down)  23.3 us
    concatenate x1, local copies, waits for them, and re-layouts, shards(): stacked = jnp.concatenate([real_part, imag_part], axis=0)  20.3 us
    all_to_all x1, waiting for transfers between devices, shards(): lax.all_to_all(stacked, 'gx', split_axis=2, concat_axis=1, tiled=True)  19.3 us
    all_to_all x2, local copies, waits for them, and re-layouts, shards(): lax.all_to_all(stacked, 'gx', split_axis=2, concat_axis=1, tiled=True)  19 us
    all_to_all x1, waiting for transfers between devices, shards(): lax.all_to_all(jnp.concatenate([back_real, back_imag], axis=0), 'gx', spl...  17.5 us
    all_to_all x1, starting transfers between devices, shards(): lax.all_to_all(stacked, 'gx', split_axis=2, concat_axis=1, tiled=True)  7.34 us
  transfers between devices with their start and end apart: 8, of which 4 were waited for; matrix products, arithmetic and copies ran while one was open for 6% of the time, Pallas kernels for 0%

commit v1 on v0

--- a/solution.py
+++ b/solution.py
@@ -6,6 +6,22 @@
 
 STEPS = 3
 HIGH = lax.Precision.HIGHEST
+
+
+def swapped_with_each(value, axis, split, join):
+    ways, here = (lax.axis_size(axis), lax.axis_index(axis))
+    width = value.shape[split] // ways
+    dims = list(value.shape)
+    dims[split] = width
+    height = dims[join]
+    dims[join] = height * ways
+    full = jnp.zeros(dims, value.dtype)
+    for mask in range(ways):
+        part = lax.dynamic_slice_in_dim(value, (here ^ mask) * width, width, axis=split)
+        if mask:
+            part = lax.ppermute(part, axis, [(d, d ^ mask) for d in range(ways)])
+        full = lax.dynamic_update_slice_in_dim(full, part, (here ^ mask) * height, axis=join)
+    return full
 
 
 def with_halo(value, sides, width):
@@ -118,7 +134,7 @@
     offset = lax.axis_index("gx") * columns
     real_part, imag_part = forward_planes(fields, cos_y, sin_y, cos_z, sin_z)
     stacked = jnp.concatenate([real_part, imag_part], axis=0)
-    lines = lax.all_to_all(stacked, "gx", split_axis=2, concat_axis=1, tiled=True)
+    lines = swapped_with_each(stacked, "gx", 2, 1)
     back_real, back_imag = line_power(lines[:2], lines[2:], cos_x, sin_x, offset)
     returned = lax.all_to_all(
         jnp.concatenate([back_real, back_imag], axis=0),

time: 313 us -> 216 us (0.69); the launches traced: 307 us -> 215 us
  local copies, waits for them, and re-layouts: 107 us -> 23.1 us
  other arithmetic: 88.9 us -> 73.2 us
  starting transfers between devices: 18 us -> 33.3 us
  waiting for transfers between devices: 60.1 us -> 49.2 us
    unnamed x11 -> x20, local copies, waits for them, and re-layouts: 60 us -> 2.7 us
    ppermute x0 -> x15, starting transfers between devices: none -> 20.8 us  [swapped_with_each(): part = lax.ppermute(part, axis, [(d, d ^ mask) for d in range(ways)])]
    concatenate x1, local copies, waits for them, and re-layouts: 20.3 us -> 0.13 us  [shards(): stacked = jnp.concatenate([real_part, imag_part], axis=0)]
    all_to_all x1 -> x0, waiting for transfers between devices: 19.3 us -> none  [shards(): lax.all_to_all(stacked, 'gx', split_axis=2, concat_axis=1, tiled=True)]
    all_to_all x2 -> x0, local copies, waits for them, and re-layouts: 19 us -> none  [shards(): lax.all_to_all(stacked, 'gx', split_axis=2, concat_axis=1, tiled=True)]
    sub x3, other arithmetic: 84 us -> 71.2 us  [advance(): total[None] - center * center]
    dynamic_update_slice x0 -> x16, local copies, waits for them, and re-layouts: none -> 10.6 us  [swapped_with_each(): lax.dynamic_update_slice_in_dim(full, part, (here ^ mask) * height, axis=...]
    all_to_all x1 -> x0, starting transfers between devices: 7.34 us -> none  [shards(): lax.all_to_all(stacked, 'gx', split_axis=2, concat_axis=1, tiled=True)]
  transfers between devices with their start and end apart: 8 -> 22, of which waited for: 4 -> 7; matrix products, arithmetic and copies ran while one was open for 6% -> 8% of each run, Pallas kernels for 0% -> 0%
where the time goes in v1:
time: 216 us; the launch traced here: 215 us
  other arithmetic  73.2 us (34%)
  waiting for transfers between devices  49.2 us (23%)
  matrix products  35.2 us (16%)
  starting transfers between devices  33.3 us (15%)
  local copies, waits for them, and re-layouts  23.1 us (11%)
    sub x3, other arithmetic, advance(): total[None] - center * center  71.2 us
    ppermute x3, waiting for transfers between devices, with_halo(): after = lax.ppermute(initial, axis, down)  28.8 us
    ppermute x15, starting transfers between devices, swapped_with_each(): part = lax.ppermute(part, axis, [(d, d ^ mask) for d in range(ways)])  20.8 us
    all_to_all x1, waiting for transfers between devices, shards(): lax.all_to_all(jnp.concatenate([back_real, back_imag], axis=0), 'gx', spl...  17.5 us
    dynamic_update_slice x16, local copies, waits for them, and re-layouts, swapped_with_each(): lax.dynamic_update_slice_in_dim(full, part, (here ^ mask) * height, axis=...  10.6 us
    all_to_all x1, starting transfers between devices, shards(): lax.all_to_all(jnp.concatenate([back_real, back_imag], axis=0), 'gx', spl...  7.1 us
    dot_general x1, matrix products, inverse_planes(): jnp.dot(imag_z, sin_y, precision=HIGH)  5.6 us
    dot_general x1, matrix products, forward_planes(): real_y = jnp.dot(fields, cos_y, precision=HIGH)  5.12 us
  transfers between devices with their start and end apart: 22, of which 7 were waited for; matrix products, arithmetic and copies ran while one was open for 8% of the time, Pallas kernels for 0%

profile of v1, /device:TPU:11, one launch (start us, length us, event | category | flops | bytes accessed | tf_op | source)
XLA Modules:
  0.0 215.2 jit_solution(718094998113069227)
XLA Ops:
  0.6 1.8 convert_add_fusion
  2.4 1.1 fusion.238
  3.5 0.7 collective-permute-start
  4.2 1.1 collective-permute-start.1
  5.3 1.6 fusion.237
  6.9 0.9 fusion.234
  8.3 1.9 multiply_subtract_fusion.2
  10.8 7.3 %collective-permute-done = f32[8,1,32,512]{3,0,2,1:T(8,128)} collective-permute-done((f32[8,1,32,512]{3,0,2,1:T(8,128)}, f32[8,1,32,512]{3,0,2,1:T(8,128)}, u32[]{:S(2)}, u32[]{:S(2)}) %collective-permute-start) | collective-permute-done | bytes 524320 | tf_op jit(solution)/shard_map/ppermute | solution.py:35
  18.1 3.4 %fusion.16 = (f32[8,3,32,512]{3,0,2,1:T(8,128)S(1)}, f32[8,3,32,512]{3,0,2,1:T(8,128)S(1)}) fusion(f32[8,3,32,512]{3,0,2,1:T(8,128)S(1)} %convert_add_fusion, f32[8,1,32,512]{3,0,2,1:T(8,128)} %collective-permute-done.1, f32[8,1,32,512]{3,0,2,1:T(8,128)} %collective-permute-done, f32[8,3,1,512]{3,0,2,1:T(8,128)S(1)} %get-tuple-element.33, ...), kind=kOutput, calls=%fused_computation.19 | convolution fusion | flops 47579328 | bytes 13828352 | tf_op jit(solution)/shard_map/gi,gxzy->ixzy/dot_general | solution.py:53
  22.3 1.8 collective-permute-start.3
  24.7 11.5 %collective-permute-done.2 = f32[8,1,32,512]{3,0,2,1:T(8,128)S(1)} collective-permute-done((f32[8,1,32,512]{3,0,2,1:T(8,128)S(1)}, f32[8,1,32,512]{3,0,2,1:T(8,128)S(1)}, u32[]{:S(2)}, u32[]{:S(2)}) %collective-permute-start.2) | collective-permute-done | bytes 524320 | tf_op jit(solution)/shard_map/ppermute | solution.py:35
  36.2 34.6 %fusion.21 = f32[8,3,32,512]{3,0,2,1:T(8,128)S(1)} fusion(f32[8,3,32,512]{3,0,2,1:T(8,128)S(1)} %get-tuple-element.56, f32[8,3,32,512]{3,0,2,1:T(8,128)S(1)} %get-tuple-element.57, f32[8,1,32,512]{3,0,2,1:T(8,128)S(1)} %collective-permute-done.3, f32[8,1,32,512]{3,0,2,1:T(8,128)S(1)} %collective-permute-done.2, f32[8,3,1,512]{3,0,2,1:T(8,128)S(1)} %get-tuple-element.23, ...), kind=kOutput, calls=%fused_computation.24 | output fusion | flops 9879559 | bytes 12058624 | tf_op jit(solution)/shard_map/sub | solution.py:63
  71.6 1.7 collective-permute-start.5
  73.9 10.0 %collective-permute-done.4 = f32[8,1,32,512]{3,0,2,1:T(8,128)S(1)} collective-permute-done((f32[8,1,32,512]{3,0,2,1:T(8,128)S(1)}, f32[8,1,32,512]{3,0,2,1:T(8,128)S(1)}, u32[]{:S(2)}, u32[]{:S(2)}) %collective-permute-start.4) | collective-permute-done | bytes 524320 | tf_op jit(solution)/shard_map/ppermute | solution.py:35
  83.9 34.6 %fusion.26 = f32[8,3,32,512]{3,0,2,1:T(8,128)S(1)} fusion(f32[8,3,32,512]{3,0,2,1:T(8,128)S(1)} %fusion.21, f32[8,3,32,512]{3,0,2,1:T(8,128)S(1)} %get-tuple-element.57, f32[8,1,32,512]{3,0,2,1:T(8,128)S(1)} %collective-permute-done.5, f32[8,1,32,512]{3,0,2,1:T(8,128)S(1)} %collective-permute-done.4, f32[8,3,1,512]{3,0,2,1:T(8,128)S(1)} %get-tuple-element.13, ...), kind=kOutput, calls=%fused_computation.29 | output fusion | flops 9879559 | bytes 12058624 | tf_op jit(solution)/shard_map/sub | solution.py:63
  118.6 0.9 fusion.169
  119.5 5.1 %convolution_negate_fusion = f32[2,3,32,512]{3,2,1,0:T(8,128)S(1)} fusion(f32[2,3,32,512]{3,0,2,1:T(2,128)S(1)} %fusion.169), kind=kOutput, calls=%fused_computation.72 | convolution fusion | flops 607748096 | bytes 786432 | tf_op jit(solution)/shard_map/dot_general | solution.py:69
  124.6 5.1 %fusion.62 = f32[2,3,32,512]{3,2,1,0:T(8,128)S(1)} fusion(f32[2,3,32,512]{3,0,2,1:T(2,128)S(1)} %fusion.169), kind=kOutput, calls=%fused_computation.86 | convolution fusion | flops 607649792 | bytes 786432 | tf_op jit(solution)/shard_map/dot_general | solution.py:68
  130.3 1.3 fusion.112
  132.5 1.6 fusion.50
  135.2 2.0 collective-permute-start.8
  137.2 2.4 %collective-permute-start.9 = (f32[4,3,1024]{2,1,0:T(4,128)S(1)}, f32[4,3,1024]{2,1,0:T(4,128)S(1)}, u32[]{:S(2)}, u32[]{:S(2)}) collective-permute-start(f32[4,3,1024]{2,1,0:T(4,128)S(1)} %get-tuple-element.49), channel_id=1, source_target_pairs={{0,4},{1,5},{2,6},{3,7},{4,0},{5,1},{6,2},{7,3},{8,12},{9,13},{10,... | collective-permute-start | bytes 147464 | tf_op jit(solution)/shard_map/ppermute | solution.py:22
  139.6 1.5 collective-permute-start.11
  141.1 1.5 collective-permute-start.12
  142.6 1.1 collective-permute-start.13
  143.7 1.2 collective-permute-start.14
  145.0 2.2 %collective-permute-start.15 = (f32[4,3,1024]{2,1,0:T(4,128)S(1)}, f32[4,3,1024]{2,1,0:T(4,128)S(1)}, u32[]{:S(2)}, u32[]{:S(2)}) collective-permute-start(f32[4,3,1024]{2,1,0:T(4,128)S(1)} %get-tuple-element.43), channel_id=1, source_target_pairs={{0,10},{1,11},{2,8},{3,9},{4,14},{5,15},{6,12},{7,13},{8,2},{9,3},... | collective-permute-start | bytes 147464 | tf_op jit(solution)/shard_map/ppermute | solution.py:22
  147.1 1.7 collective-permute-start.16
  148.8 0.7 collective-permute-start.17
  149.6 3.3 %collective-permute-start.18 = (f32[4,3,1024]{2,1,0:T(4,128)S(1)}, f32[4,3,1024]{2,1,0:T(4,128)}, u32[]{:S(2)}, u32[]{:S(2)}) collective-permute-start(f32[4,3,1024]{2,1,0:T(4,128)S(1)} %get-tuple-element.40), channel_id=1, source_target_pairs={{0,13},{1,12},{2,15},{3,14},{4,9},{5,8},{6,11},{7,10},{8,5},{9,4},... | collective-permute-start | bytes 147464 | tf_op jit(solution)/shard_map/ppermute | solution.py:22
  152.9 0.8 collective-permute-done.14
  153.8 0.7 collective-permute-start.19
  154.5 0.7 collective-permute-done.15
  155.2 2.2 %collective-permute-start.20 = (f32[4,3,1024]{2,1,0:T(4,128)S(1)}, f32[4,3,1024]{2,1,0:T(4,128)}, u32[]{:S(2)}, u32[]{:S(2)}) collective-permute-start(f32[4,3,1024]{2,1,0:T(4,128)S(1)} %get-tuple-element.38), channel_id=1, source_target_pairs={{0,15},{1,14},{2,13},{3,12},{4,11},{5,10},{6,9},{7,8},{8,7},{9,6},... | collective-permute-start | bytes 147464 | tf_op jit(solution)/shard_map/ppermute | solution.py:22
  161.4 1.1 dynamic_update_slice.58
  162.5 1.1 dynamic_update_slice.59
  163.6 1.1 dynamic_update_slice.60
  164.8 1.3 collective-permute-done.18
  166.1 1.1 dynamic_update_slice.61
  167.2 1.1 dynamic_update_slice.62
  168.3 1.3 dynamic_update_slice.63
  171.6 0.7 fusion.55
  173.5 1.4 copy.47
  174.9 7.1 %all-to-all-start = ((f32[4,48,1024]{2,0,1:T(4,128)}), f32[4,48,1024]{2,0,1:T(4,128)S(1)}, u32[]{:S(2)}, u32[]{:S(2)}) async-start(f32[4,48,1024]{2,0,1:T(4,128)} %copy.47), calls=%async_computation | async-start | bytes 1572864 | tf_op jit(solution)/shard_map/all_to_all | solution.py:139
  182.0 2.1 copy.50
  184.1 17.5 %all-to-all-done = f32[4,48,1024]{2,0,1:T(4,128)S(1)} async-done(((f32[4,48,1024]{2,0,1:T(4,128)}), f32[4,48,1024]{2,0,1:T(4,128)S(1)}, u32[]{:S(2)}, u32[]{:S(2)}) %all-to-all-start) | async-done | bytes 786464 | tf_op jit(solution)/shard_map/all_to_all | solution.py:139
  204.5 5.1 %fusion.60 = f32[2,3,32,512]{3,2,1,0:T(8,128)S(1)} fusion(f32[2,3,32,512]{3,2,1,0:T(8,128)S(1)} %fusion.48), kind=kOutput, calls=%fused_computation.84 | convolution fusion | flops 607649792 | bytes 786432 | tf_op jit(solution)/shard_map/dot_general | solution.py:111
  209.6 5.6 %fusion.56 = f32[2,3,32,512]{3,2,1,0:T(8,128)} fusion(f32[2,3,32,512]{3,2,1,0:T(8,128)S(1)} %fusion.60, f32[2,3,32,512]{3,2,1,0:T(8,128)S(1)} %fusion.47), kind=kOutput, calls=%fused_computation.80 | convolution fusion | flops 607846400 | bytes 1179648 | tf_op jit(solution)/shard_map/dot_general | solution.py:111
  (86 shorter events, 16.1 us)
Async XLA Ops:
  3.5 14.6 %collective-permute-start = (f32[8,1,32,512]{3,0,2,1:T(8,128)}, f32[8,1,32,512]{3,0,2,1:T(8,128)}, u32[]{:S(2)}, u32[]{:S(2)}) collective-permute-start(f32[8,1,32,512]{3,0,2,1:T(8,128)} %get-tuple-element.36), channel_id=1, source_target_pairs={{1,0},{2,1},{3,2},{4,3},{5,4},{6,5},{7,6},{8,7},{9,8},{10,9},{11,1... | collective-permute-start | bytes 1572872 | tf_op jit(solution)/shard_map/ppermute | solution.py:35
  4.2 13.9 %collective-permute-start.1 = (f32[8,1,32,512]{3,0,2,1:T(8,128)}, f32[8,1,32,512]{3,0,2,1:T(8,128)}, u32[]{:S(2)}, u32[]{:S(2)}) collective-permute-start(f32[8,1,32,512]{3,0,2,1:T(8,128)} %get-tuple-element.37), channel_id=1, source_target_pairs={{0,1},{1,2},{2,3},{3,4},{4,5},{5,6},{6,7},{7,8},{8,9},{9,10},{10,1... | collective-permute-start | bytes 1572872 | tf_op jit(solution)/shard_map/ppermute | solution.py:34
  6.9 0.9 copy-start.3
  6.9 1.4 copy-start.5
  10.2 7.9 %copy-start = (f32[8,3,31,512]{3,0,2,1:T(8,128)S(1)}, f32[8,3,31,512]{3,0,2,1:T(8,128)}, u32[]{:S(2)}) copy-start(f32[8,3,31,512]{3,0,2,1:T(8,128)} %get-tuple-element.35) | copy-start | bytes 4571140
  10.2 7.9 %copy-start.1 = (f32[8,3,32,512]{3,0,2,1:T(8,128)S(1)}, f32[8,3,32,512]{3,0,2,1:T(8,128)}, u32[]{:S(2)}) copy-start(f32[8,3,32,512]{3,0,2,1:T(8,128)} %multiply_subtract_fusion.2) | copy-start | bytes 4718596
  10.2 7.9 %copy-start.2 = (f32[8,3,32,1]{3,0,2,1:T(8,128)S(1)}, f32[8,3,32,1]{3,0,2,1:T(8,128)}, u32[]{:S(2)}) copy-start(f32[8,3,32,1]{3,0,2,1:T(8,128)} %get-tuple-element.29) | copy-start | bytes 9220
  10.2 7.9 %copy-start.4 = (s32[3,32,512]{2,1,0:T(8,128)S(1)}, s32[3,32,512]{2,1,0:T(8,128)}, u32[]{:S(2)}) copy-start(s32[3,32,512]{2,1,0:T(8,128)} %param.4) | copy-start | bytes 589828
  10.3 7.9 %copy-start.7 = (s32[8,8]{1,0:T(8,128)S(1)}, s32[8,8]{1,0:T(8,128)}, u32[]{:S(2)}) copy-start(s32[8,8]{1,0:T(8,128)} %param.6) | copy-start | bytes 772
  22.2 14.0 %collective-permute-start.2 = (f32[8,1,32,512]{3,0,2,1:T(8,128)S(1)}, f32[8,1,32,512]{3,0,2,1:T(8,128)S(1)}, u32[]{:S(2)}, u32[]{:S(2)}) collective-permute-start(f32[8,1,32,512]{3,0,2,1:T(8,128)S(1)} %get-tuple-element.26), channel_id=1, source_target_pairs={{1,0},{2,1},{3,2},{4,3},{5,4},{6,5},{7,6},{8,7},{9,8},{10,9},{11,1... | collective-permute-start | bytes 1572872 | tf_op jit(solution)/shard_map/ppermute | solution.py:35
  22.3 13.9 %collective-permute-start.3 = (f32[8,1,32,512]{3,0,2,1:T(8,128)S(1)}, f32[8,1,32,512]{3,0,2,1:T(8,128)S(1)}, u32[]{:S(2)}, u32[]{:S(2)}) collective-permute-start(f32[8,1,32,512]{3,0,2,1:T(8,128)S(1)} %get-tuple-element.27), channel_id=1, source_target_pairs={{0,1},{1,2},{2,3},{3,4},{4,5},{5,6},{6,7},{7,8},{8,9},{9,10},{10,1... | collective-permute-start | bytes 1572872 | tf_op jit(solution)/shard_map/ppermute | solution.py:34
  71.5 12.4 %collective-permute-start.4 = (f32[8,1,32,512]{3,0,2,1:T(8,128)S(1)}, f32[8,1,32,512]{3,0,2,1:T(8,128)S(1)}, u32[]{:S(2)}, u32[]{:S(2)}) collective-permute-start(f32[8,1,32,512]{3,0,2,1:T(8,128)S(1)} %get-tuple-element.16), channel_id=1, source_target_pairs={{1,0},{2,1},{3,2},{4,3},{5,4},{6,5},{7,6},{8,7},{9,8},{10,9},{11,1... | collective-permute-start | bytes 1572872 | tf_op jit(solution)/shard_map/ppermute | solution.py:35
  71.6 12.3 %collective-permute-start.5 = (f32[8,1,32,512]{3,0,2,1:T(8,128)S(1)}, f32[8,1,32,512]{3,0,2,1:T(8,128)S(1)}, u32[]{:S(2)}, u32[]{:S(2)}) collective-permute-start(f32[8,1,32,512]{3,0,2,1:T(8,128)S(1)} %get-tuple-element.17), channel_id=1, source_target_pairs={{0,1},{1,2},{2,3},{3,4},{4,5},{5,6},{6,7},{7,8},{8,9},{9,10},{10,1... | collective-permute-start | bytes 1572872 | tf_op jit(solution)/shard_map/ppermute | solution.py:34
  83.9 34.7 %copy-start.8 = (s32[2]{0:T(128)S(1)}, s32[2]{0:T(128)}, u32[]{:S(2)}) copy-start(s32[2]{0:T(128)} %param.7) | copy-start | bytes 28
  135.0 4.6 %collective-permute-start.6 = (f32[4,3,1024]{2,1,0:T(4,128)S(1)}, f32[4,3,1024]{2,1,0:T(4,128)S(1)}, u32[]{:S(2)}, u32[]{:S(2)}) collective-permute-start(f32[4,3,1024]{2,1,0:T(4,128)S(1)} %get-tuple-element.52), channel_id=1, source_target_pairs={{0,1},{1,0},{2,3},{3,2},{4,5},{5,4},{6,7},{7,6},{8,9},{9,8},{10,11... | collective-permute-start | bytes 147464 | tf_op jit(solution)/shard_map/ppermute | solution.py:22
  135.1 6.0 %collective-permute-start.7 = (f32[4,3,1024]{2,1,0:T(4,128)S(1)}, f32[4,3,1024]{2,1,0:T(4,128)S(1)}, u32[]{:S(2)}, u32[]{:S(2)}) collective-permute-start(f32[4,3,1024]{2,1,0:T(4,128)S(1)} %get-tuple-element.51), channel_id=1, source_target_pairs={{0,2},{1,3},{2,0},{3,1},{4,6},{5,7},{6,4},{7,5},{8,10},{9,11},{10,... | collective-permute-start | bytes 147464 | tf_op jit(solution)/shard_map/ppermute | solution.py:22
  135.2 7.5 %collective-permute-start.8 = (f32[4,3,1024]{2,1,0:T(4,128)S(1)}, f32[4,3,1024]{2,1,0:T(4,128)S(1)}, u32[]{:S(2)}, u32[]{:S(2)}) collective-permute-start(f32[4,3,1024]{2,1,0:T(4,128)S(1)} %get-tuple-element.50), channel_id=1, source_target_pairs={{0,3},{1,2},{2,1},{3,0},{4,7},{5,6},{6,5},{7,4},{8,11},{9,10},{10,... | collective-permute-start | bytes 147464 | tf_op jit(solution)/shard_map/ppermute | solution.py:22
  137.2 6.5 %collective-permute-start.9 = (f32[4,3,1024]{2,1,0:T(4,128)S(1)}, f32[4,3,1024]{2,1,0:T(4,128)S(1)}, u32[]{:S(2)}, u32[]{:S(2)}) collective-permute-start(f32[4,3,1024]{2,1,0:T(4,128)S(1)} %get-tuple-element.49), channel_id=1, source_target_pairs={{0,4},{1,5},{2,6},{3,7},{4,0},{5,1},{6,2},{7,3},{8,12},{9,13},{10,... | collective-permute-start | bytes 147464 | tf_op jit(solution)/shard_map/ppermute | solution.py:22
  139.6 5.4 %collective-permute-start.10 = (f32[4,3,1024]{2,1,0:T(4,128)S(1)}, f32[4,3,1024]{2,1,0:T(4,128)S(1)}, u32[]{:S(2)}, u32[]{:S(2)}) collective-permute-start(f32[4,3,1024]{2,1,0:T(4,128)S(1)} %get-tuple-element.48), channel_id=1, source_target_pairs={{0,5},{1,4},{2,7},{3,6},{4,1},{5,0},{6,3},{7,2},{8,13},{9,12},{10,... | collective-permute-start | bytes 147464 | tf_op jit(solution)/shard_map/ppermute | solution.py:22
  139.6 7.5 %collective-permute-start.11 = (f32[4,3,1024]{2,1,0:T(4,128)S(1)}, f32[4,3,1024]{2,1,0:T(4,128)S(1)}, u32[]{:S(2)}, u32[]{:S(2)}) collective-permute-start(f32[4,3,1024]{2,1,0:T(4,128)S(1)} %get-tuple-element.47), channel_id=1, source_target_pairs={{0,6},{1,7},{2,4},{3,5},{4,2},{5,3},{6,0},{7,1},{8,14},{9,15},{10,... | collective-permute-start | bytes 147464 | tf_op jit(solution)/shard_map/ppermute | solution.py:22
  141.1 7.7 %collective-permute-start.12 = (f32[4,3,1024]{2,1,0:T(4,128)S(1)}, f32[4,3,1024]{2,1,0:T(4,128)S(1)}, u32[]{:S(2)}, u32[]{:S(2)}) collective-permute-start(f32[4,3,1024]{2,1,0:T(4,128)S(1)} %get-tuple-element.46), channel_id=1, source_target_pairs={{0,7},{1,6},{2,5},{3,4},{4,3},{5,2},{6,1},{7,0},{8,15},{9,14},{10,... | collective-permute-start | bytes 147464 | tf_op jit(solution)/shard_map/ppermute | solution.py:22
  142.6 7.0 %collective-permute-start.13 = (f32[4,3,1024]{2,1,0:T(4,128)S(1)}, f32[4,3,1024]{2,1,0:T(4,128)S(1)}, u32[]{:S(2)}, u32[]{:S(2)}) collective-permute-start(f32[4,3,1024]{2,1,0:T(4,128)S(1)} %get-tuple-element.45), channel_id=1, source_target_pairs={{0,8},{1,9},{2,10},{3,11},{4,12},{5,13},{6,14},{7,15},{8,0},{9,1},... | collective-permute-start | bytes 147464 | tf_op jit(solution)/shard_map/ppermute | solution.py:22
  143.7 10.0 %collective-permute-start.14 = (f32[4,3,1024]{2,1,0:T(4,128)S(1)}, f32[4,3,1024]{2,1,0:T(4,128)S(1)}, u32[]{:S(2)}, u32[]{:S(2)}) collective-permute-start(f32[4,3,1024]{2,1,0:T(4,128)S(1)} %get-tuple-element.44), channel_id=1, source_target_pairs={{0,9},{1,8},{2,11},{3,10},{4,13},{5,12},{6,15},{7,14},{8,1},{9,0},... | collective-permute-start | bytes 147464 | tf_op jit(solution)/shard_map/ppermute | solution.py:22
  145.0 10.2 %collective-permute-start.15 = (f32[4,3,1024]{2,1,0:T(4,128)S(1)}, f32[4,3,1024]{2,1,0:T(4,128)S(1)}, u32[]{:S(2)}, u32[]{:S(2)}) collective-permute-start(f32[4,3,1024]{2,1,0:T(4,128)S(1)} %get-tuple-element.43), channel_id=1, source_target_pairs={{0,10},{1,11},{2,8},{3,9},{4,14},{5,15},{6,12},{7,13},{8,2},{9,3},... | collective-permute-start | bytes 147464 | tf_op jit(solution)/shard_map/ppermute | solution.py:22
  147.1 15.4 %collective-permute-start.16 = (f32[4,3,1024]{2,1,0:T(4,128)S(1)}, f32[4,3,1024]{2,1,0:T(4,128)}, u32[]{:S(2)}, u32[]{:S(2)}) collective-permute-start(f32[4,3,1024]{2,1,0:T(4,128)S(1)} %get-tuple-element.42), channel_id=1, source_target_pairs={{0,11},{1,10},{2,9},{3,8},{4,15},{5,14},{6,13},{7,12},{8,3},{9,2},... | collective-permute-start | bytes 147464 | tf_op jit(solution)/shard_map/ppermute | solution.py:22
  148.8 14.8 %collective-permute-start.17 = (f32[4,3,1024]{2,1,0:T(4,128)S(1)}, f32[4,3,1024]{2,1,0:T(4,128)}, u32[]{:S(2)}, u32[]{:S(2)}) collective-permute-start(f32[4,3,1024]{2,1,0:T(4,128)S(1)} %get-tuple-element.41), channel_id=1, source_target_pairs={{0,12},{1,13},{2,14},{3,15},{4,8},{5,9},{6,10},{7,11},{8,4},{9,5},... | collective-permute-start | bytes 147464 | tf_op jit(solution)/shard_map/ppermute | solution.py:22
  149.6 16.5 %collective-permute-start.18 = (f32[4,3,1024]{2,1,0:T(4,128)S(1)}, f32[4,3,1024]{2,1,0:T(4,128)}, u32[]{:S(2)}, u32[]{:S(2)}) collective-permute-start(f32[4,3,1024]{2,1,0:T(4,128)S(1)} %get-tuple-element.40), channel_id=1, source_target_pairs={{0,13},{1,12},{2,15},{3,14},{4,9},{5,8},{6,11},{7,10},{8,5},{9,4},... | collective-permute-start | bytes 147464 | tf_op jit(solution)/shard_map/ppermute | solution.py:22
  153.8 13.4 %collective-permute-start.19 = (f32[4,3,1024]{2,1,0:T(4,128)S(1)}, f32[4,3,1024]{2,1,0:T(4,128)}, u32[]{:S(2)}, u32[]{:S(2)}) collective-permute-start(f32[4,3,1024]{2,1,0:T(4,128)S(1)} %get-tuple-element.39), channel_id=1, source_target_pairs={{0,14},{1,15},{2,12},{3,13},{4,10},{5,11},{6,8},{7,9},{8,6},{9,7},... | collective-permute-start | bytes 147464 | tf_op jit(solution)/shard_map/ppermute | solution.py:22
  155.2 2.2 %copy-start.6 = (f32[4,3,1024]{2,1,0:T(4,128)}, f32[4,3,1024]{2,1,0:T(4,128)S(1)}, u32[]{:S(2)}) copy-start(f32[4,3,1024]{2,1,0:T(4,128)S(1)} %collective-permute-done.15) | copy-start | bytes 147460
  155.2 13.2 %collective-permute-start.20 = (f32[4,3,1024]{2,1,0:T(4,128)S(1)}, f32[4,3,1024]{2,1,0:T(4,128)}, u32[]{:S(2)}, u32[]{:S(2)}) collective-permute-start(f32[4,3,1024]{2,1,0:T(4,128)S(1)} %get-tuple-element.38), channel_id=1, source_target_pairs={{0,15},{1,14},{2,13},{3,12},{4,11},{5,10},{6,9},{7,8},{8,7},{9,6},... | collective-permute-start | bytes 147464 | tf_op jit(solution)/shard_map/ppermute | solution.py:22
  174.9 26.7 %all-to-all-start = ((f32[4,48,1024]{2,0,1:T(4,128)}), f32[4,48,1024]{2,0,1:T(4,128)S(1)}, u32[]{:S(2)}, u32[]{:S(2)}) async-start(f32[4,48,1024]{2,0,1:T(4,128)} %copy.47), calls=%async_computation | async-start | bytes 1572864 | tf_op jit(solution)/shard_map/all_to_all | solution.py:139
